TPU v7x, 32 devices: a whole 2x2x4 slice. The times are simulated.
32 devices in a mesh: dp: 8 (over y, x, core), seq: 4 (over z).
Axes of the slice: x: 2, y: 2, z: 4, core: 2. Of those that a mesh axis runs over, the one named last changes fastest.
Arguments:
- inputs: bfloat16 [24, 1024, 768], P('dp', 'seq'), may hold values from -6 to 6
- cotangent: bfloat16 [24, 1024, 768], P('dp', 'seq'), may hold values from -6 to 6
- lengths: int32 [24], P('dp'), may hold values from 100 to 1024, as said below
- predicted: int32 [24, 1024], P('dp', 'seq'), may hold values from 0 to 69
- norm1_gain: float32 [768], replicated, may hold values from 0.1 to 1.9
- norm1_shift: float32 [768], replicated, may hold values from -4 to 4
- w_query: bfloat16 [768, 768], replicated, may hold values from -0.3125 to 0.3125
- b_query: float32 [768], replicated, may hold values from -6 to 6
- w_key: bfloat16 [768, 768], replicated, may hold values from -0.3125 to 0.3125
- b_key: float32 [768], replicated, may hold values from -6 to 6
- w_value: bfloat16 [768, 768], replicated, may hold values from -0.21875 to 0.21875
- b_value: float32 [768], replicated, may hold values from -6 to 6
- w_out: bfloat16 [768, 768], replicated, may hold values from -2 to 2
- b_out: float32 [768], replicated, may hold values from -6 to 6
- norm2_gain: float32 [768], replicated, may hold values from 0.1 to 1.9
- norm2_shift: float32 [768], replicated, may hold values from -4 to 4
- w_up: bfloat16 [768, 3072], replicated, may hold values from -0.21875 to 0.21875
- b_up: float32 [3072], replicated, may hold values from -6 to 6
- w_down: bfloat16 [3072, 768], replicated, may hold values from -0.109375 to 0.109375
- b_down: float32 [768], replicated, may hold values from -6 to 6
Outputs:
- result: bfloat16 [24, 1024, 768], P('dp', 'seq')
- grad_inputs: bfloat16 [24, 1024, 768], P('dp', 'seq')
- grad_norm1_gain: float32 [768], replicated
- grad_norm1_shift: float32 [768], replicated
- grad_w_query: float32 [768, 768], replicated
- grad_b_query: float32 [768], replicated
- grad_w_key: float32 [768, 768], replicated
- grad_b_key: float32 [768], replicated
- grad_w_value: float32 [768, 768], replicated
- grad_b_value: float32 [768], replicated
- grad_w_out: float32 [768, 768], replicated
- grad_b_out: float32 [768], replicated
- grad_norm2_gain: float32 [768], replicated
- grad_norm2_shift: float32 [768], replicated
- grad_w_up: float32 [768, 3072], replicated
- grad_b_up: float32 [3072], replicated
- grad_w_down: float32 [3072, 768], replicated
- grad_b_down: float32 [768], replicated
- histogram: int32 [70], replicated
Inputs may be any that keep to these rules, and one draw needn't show every extreme that they name: Some sequence has 1024 real codons and some has 100; the codons from position lengths[s] on are padding.
All inputs are finite; a program needn't handle non-finite values.
Results may differ from a plain program's by a relative error of at most 0.014.
The roundings to bfloat16 on the way count: a program that leaves them out, or rounds other values in their place, can miss the bound.
Values may be sent and summed in bfloat16 or wider, within the bound.
No kernel may reach another device: no remote copies, remote signals or barrier semaphores. Data moves between devices by JAX's collectives and lax.ppermute only.
A program may use at most 192 MiB of HBM per device.

v0:
```python
import jax
import jax.numpy as jnp
from jax import lax
from jax.sharding import PartitionSpec as P

HEAD = 64
CLASSES = 70
epsilon = 1e-05


def matmul(left, right):
    return jnp.dot(left, right, preferred_element_type=jnp.float32)


def matmul_left(left, right):
    return lax.dot_general(
        left, right, (((0,), (0,)), ((), ())), preferred_element_type=jnp.float32
    )


def matmul_right(left, right):
    return lax.dot_general(
        left, right, (((1,), (1,)), ((), ())), preferred_element_type=jnp.float32
    )


def layer_norm(value, gain, shift):
    centre = value - jnp.mean(value, axis=-1, keepdims=True)
    scale = lax.rsqrt(jnp.mean(centre * centre, axis=-1, keepdims=True) + epsilon)
    return centre * scale * gain + shift


def gelu(value):
    return jax.nn.gelu(value, approximate=False)


def rotate(value, direction):
    count = value.shape[-3]
    half = value.shape[-1] // 2
    frequency = 10000.0 ** (-jnp.arange(half, dtype=jnp.float32) / half)
    angle = jnp.arange(count, dtype=jnp.float32)[:, None] * frequency[None, :]
    cosine = jnp.cos(angle)[:, None, :]
    sine = direction * jnp.sin(angle)[:, None, :]
    first = value[..., :half]
    second = value[..., half:]
    return jnp.concatenate(
        [first * cosine - second * sine, second * cosine + first * sine], axis=-1
    )


def attend_forward(query, key, value, valid, block):
    count, heads, size = query.shape
    scale = HEAD ** (-0.5)
    blocks = query.reshape(count // block, block, heads, size)

    def visit(query_block):
        scores = (
            jnp.einsum("qhd,khd->hqk", query_block, key, preferred_element_type=jnp.float32) * scale
        )
        scores = jnp.where(valid[None, None, :], scores, -1e30)
        peak = jnp.max(scores, axis=-1, keepdims=True)
        total = jnp.sum(jnp.exp(scores - peak), axis=-1, keepdims=True)
        logsum = peak + jnp.log(total)
        weights = jnp.exp(scores - logsum).astype(jnp.bfloat16)
        mixed = jnp.einsum("hqk,khd->qhd", weights, value, preferred_element_type=jnp.float32)
        return (mixed.astype(jnp.bfloat16), logsum[..., 0])

    mixed, logsum = lax.map(visit, blocks)
    return (mixed.reshape(count, heads * size), logsum)


def attend_backward(query, key, value, valid, logsum, grad_mixed, block):
    count, heads, size = query.shape
    number = count // block
    scale = HEAD ** (-0.5)
    query_blocks = query.reshape(number, block, heads, size)
    grad_blocks = grad_mixed.reshape(number, block, heads, size)

    def visit(carry, item):
        grad_key, grad_value = carry
        query_block, grad_block, logsum_block = item
        scores = (
            jnp.einsum("qhd,khd->hqk", query_block, key, preferred_element_type=jnp.float32) * scale
        )
        scores = jnp.where(valid[None, None, :], scores, -1e30)
        weights = jnp.exp(scores - logsum_block[..., None])
        weights_low = weights.astype(jnp.bfloat16)
        grad_weights = jnp.einsum(
            "qhd,khd->hqk", grad_block, value, preferred_element_type=jnp.float32
        )
        inner = jnp.sum(weights * grad_weights, axis=-1, keepdims=True)
        grad_scores = (weights * (grad_weights - inner)).astype(jnp.bfloat16)
        grad_query = (
            jnp.einsum("hqk,khd->qhd", grad_scores, key, preferred_element_type=jnp.float32) * scale
        )
        grad_key = (
            grad_key
            + jnp.einsum(
                "hqk,qhd->khd", grad_scores, query_block, preferred_element_type=jnp.float32
            )
            * scale
        )
        grad_value = grad_value + jnp.einsum(
            "hqk,qhd->khd", weights_low, grad_block, preferred_element_type=jnp.float32
        )
        return ((grad_key, grad_value), grad_query)

    start = jnp.zeros((count, heads, size), jnp.float32)
    (grad_key, grad_value), grad_query = lax.scan(
        visit, (start, start), (query_blocks, grad_blocks, logsum)
    )
    grad_query = rotate(grad_query.reshape(count, heads, size), -1.0).astype(jnp.bfloat16)
    grad_key = rotate(grad_key, -1.0).astype(jnp.bfloat16)
    grad_value = grad_value.astype(jnp.bfloat16)
    return (
        grad_query.reshape(count, heads * size),
        grad_key.reshape(count, heads * size),
        grad_value.reshape(count, heads * size),
    )


def on_device(
    inputs,
    cotangent,
    lengths,
    predicted,
    norm1_gain,
    norm1_shift,
    w_query,
    b_query,
    w_key,
    b_key,
    w_value,
    b_value,
    w_out,
    b_out,
    norm2_gain,
    norm2_shift,
    w_up,
    b_up,
    w_down,
    b_down,
):
    seqs, span, width = inputs.shape
    tokens = seqs * span
    hidden_width = w_up.shape[1]
    flat_in = inputs.reshape(tokens, width).astype(jnp.float32)
    normed_full, norm1_back = jax.vjp(layer_norm, flat_in, norm1_gain, norm1_shift)
    normed = normed_full.astype(jnp.bfloat16)
    query = (matmul(normed, w_query) + b_query).astype(jnp.bfloat16).reshape(seqs, span, width)
    key = (matmul(normed, w_key) + b_key).astype(jnp.bfloat16).reshape(seqs, span, width)
    value = (matmul(normed, w_value) + b_value).astype(jnp.bfloat16).reshape(seqs, span, width)
    head_query, head_key, head_value = (
        lax.all_to_all(query, "seq", split_axis=2, concat_axis=1, tiled=True),
        lax.all_to_all(key, "seq", split_axis=2, concat_axis=1, tiled=True),
        lax.all_to_all(value, "seq", split_axis=2, concat_axis=1, tiled=True),
    )
    count = head_query.shape[1]
    heads = head_query.shape[2] // HEAD
    shaped = (seqs, count, heads, HEAD)
    rot_query = rotate(head_query.reshape(shaped).astype(jnp.float32), 1.0).astype(jnp.bfloat16)
    rot_key = rotate(head_key.reshape(shaped).astype(jnp.float32), 1.0).astype(jnp.bfloat16)
    head_value = head_value.reshape(shaped)
    valid = jnp.arange(count)[None, :] < lengths[:, None]
    block = min(count, 512)
    mixed, logsum = lax.map(
        lambda item: attend_forward(item[0], item[1], item[2], item[3], block),
        (rot_query, rot_key, head_value, valid),
    )
    attended = lax.all_to_all(mixed, "seq", split_axis=1, concat_axis=2, tiled=True).reshape(
        tokens, width
    )
    middle = flat_in + matmul(attended, w_out) + b_out
    normed2_full, norm2_back = jax.vjp(layer_norm, middle, norm2_gain, norm2_shift)
    normed2 = normed2_full.astype(jnp.bfloat16)
    hidden_in = matmul(normed2, w_up) + b_up
    hidden = gelu(hidden_in).astype(jnp.bfloat16)
    result = (
        (middle + matmul(hidden, w_down) + b_down).astype(jnp.bfloat16).reshape(seqs, span, width)
    )
    grad_result = cotangent.reshape(tokens, width)
    grad_result_full = grad_result.astype(jnp.float32)
    grad_w_down = matmul_left(hidden, grad_result)
    grad_b_down = jnp.sum(grad_result_full, axis=0)
    unused, gelu_back = jax.vjp(gelu, hidden_in)
    grad_hidden_in = gelu_back(matmul_right(grad_result, w_down))[0].astype(jnp.bfloat16)
    grad_w_up = matmul_left(normed2, grad_hidden_in)
    grad_b_up = jnp.sum(grad_hidden_in.astype(jnp.float32), axis=0)
    grad_from_norm2, grad_norm2_gain, grad_norm2_shift = norm2_back(
        matmul_right(grad_hidden_in, w_up)
    )
    grad_middle = grad_result_full + grad_from_norm2
    grad_branch = grad_middle.astype(jnp.bfloat16)
    grad_w_out = matmul_left(attended, grad_branch)
    grad_b_out = jnp.sum(grad_middle, axis=0)
    grad_attended = matmul_right(grad_branch, w_out).astype(jnp.bfloat16).reshape(seqs, span, width)
    grad_mixed = lax.all_to_all(
        grad_attended, "seq", split_axis=2, concat_axis=1, tiled=True
    ).reshape(shaped)
    grad_query, grad_key, grad_value = lax.map(
        lambda item: attend_backward(item[0], item[1], item[2], item[3], item[4], item[5], block),
        (rot_query, rot_key, head_value, valid, logsum, grad_mixed),
    )
    back_query, back_key, back_value = (
        lax.all_to_all(grad_query, "seq", split_axis=1, concat_axis=2, tiled=True),
        lax.all_to_all(grad_key, "seq", split_axis=1, concat_axis=2, tiled=True),
        lax.all_to_all(grad_value, "seq", split_axis=1, concat_axis=2, tiled=True),
    )
    back_query = back_query.reshape(tokens, width)
    back_key = back_key.reshape(tokens, width)
    back_value = back_value.reshape(tokens, width)
    grad_w_query = matmul_left(normed, back_query)
    grad_w_key = matmul_left(normed, back_key)
    grad_w_value = matmul_left(normed, back_value)
    grad_b_query = jnp.sum(back_query.astype(jnp.float32), axis=0)
    grad_b_key = jnp.sum(back_key.astype(jnp.float32), axis=0)
    grad_b_value = jnp.sum(back_value.astype(jnp.float32), axis=0)
    grad_normed = (
        matmul_right(back_query, w_query)
        + matmul_right(back_key, w_key)
        + matmul_right(back_value, w_value)
    )
    grad_from_norm1, grad_norm1_gain, grad_norm1_shift = norm1_back(grad_normed)
    grad_inputs = (grad_middle + grad_from_norm1).astype(jnp.bfloat16).reshape(seqs, span, width)
    position = lax.axis_index("seq") * span + jnp.arange(span)
    live = position[None, :] < lengths[:, None]
    classes = jnp.arange(CLASSES)
    counts = jnp.sum(
        jnp.where(live[:, :, None] & (predicted[:, :, None] == classes), 1.0, 0.0), axis=(0, 1)
    )
    (
        grad_norm1_gain,
        grad_norm1_shift,
        grad_b_query,
        grad_b_key,
        grad_b_value,
        grad_b_out,
        grad_norm2_gain,
        grad_norm2_shift,
        grad_b_up,
        grad_b_down,
        counts,
    ) = lax.psum(
        (
            grad_norm1_gain,
            grad_norm1_shift,
            grad_b_query,
            grad_b_key,
            grad_b_value,
            grad_b_out,
            grad_norm2_gain,
            grad_norm2_shift,
            grad_b_up,
            grad_b_down,
            counts,
        ),
        ("dp", "seq"),
    )
    part_query = grad_w_query.reshape(-1)
    part_key = grad_w_key.reshape(-1)
    part_value = grad_w_value.reshape(-1)
    part_out = grad_w_out.reshape(-1)
    part_up = grad_w_up.reshape(-1)
    part_down = grad_w_down.reshape(-1)
    part_query, part_key, part_value, part_out, part_up, part_down = (
        lax.psum_scatter(part_query, ("dp", "seq"), scatter_dimension=0, tiled=True),
        lax.psum_scatter(part_key, ("dp", "seq"), scatter_dimension=0, tiled=True),
        lax.psum_scatter(part_value, ("dp", "seq"), scatter_dimension=0, tiled=True),
        lax.psum_scatter(part_out, ("dp", "seq"), scatter_dimension=0, tiled=True),
        lax.psum_scatter(part_up, ("dp", "seq"), scatter_dimension=0, tiled=True),
        lax.psum_scatter(part_down, ("dp", "seq"), scatter_dimension=0, tiled=True),
    )
    part_query, part_key, part_value, part_out, part_up, part_down = (
        lax.all_gather(part_query, ("dp", "seq"), axis=0, tiled=True),
        lax.all_gather(part_key, ("dp", "seq"), axis=0, tiled=True),
        lax.all_gather(part_value, ("dp", "seq"), axis=0, tiled=True),
        lax.all_gather(part_out, ("dp", "seq"), axis=0, tiled=True),
        lax.all_gather(part_up, ("dp", "seq"), axis=0, tiled=True),
        lax.all_gather(part_down, ("dp", "seq"), axis=0, tiled=True),
    )
    return (
        result,
        grad_inputs,
        grad_norm1_gain,
        grad_norm1_shift,
        part_query.reshape(width, width),
        grad_b_query,
        part_key.reshape(width, width),
        grad_b_key,
        part_value.reshape(width, width),
        grad_b_value,
        part_out.reshape(width, width),
        grad_b_out,
        grad_norm2_gain,
        grad_norm2_shift,
        part_up.reshape(width, hidden_width),
        grad_b_up,
        part_down.reshape(hidden_width, width),
        grad_b_down,
        counts.astype(jnp.int32),
    )


def solution(mesh):
    return jax.shard_map(
        on_device,
        mesh=mesh,
        in_specs=(
            P("dp", "seq", None),
            P("dp", "seq", None),
            P("dp"),
            P("dp", "seq"),
            P(),
            P(),
            P(),
            P(),
            P(),
            P(),
            P(),
            P(),
            P(),
            P(),
            P(),
            P(),
            P(),
            P(),
            P(),
            P(),
        ),
        out_specs=(
            P("dp", "seq", None),
            P("dp", "seq", None),
            P(),
            P(),
            P(),
            P(),
            P(),
            P(),
            P(),
            P(),
            P(),
            P(),
            P(),
            P(),
            P(),
            P(),
            P(),
            P(),
            P(),
        ),
        check_vma=False,
    )
```

profile of v0, /device:TPU:0, one launch (start us, length us, event | category | flops | bytes accessed | tf_op | source)
XLA Modules:
  0.0 1592.5 jit_solution(14903146880478550544)
XLA Ops:
  29.5 29.6 %all-to-all-done.1 = bf16[3,256,768]{1,0,2:T(4,128)(2,1)S(1)} async-done(((bf16[3,256,768]{1,0,2:T(4,128)(2,1)}), bf16[3,256,768]{1,0,2:T(4,128)(2,1)S(1)}, u32[]{:S(2)}, u32[]{:S(2)}) %all-to-all-start.1) | async-done | bytes 1179680 | tf_op jit(solution)/shard_map/all_to_all | solution.py:155
  70.5 29.5 %all-to-all-done = bf16[3,256,768]{1,0,2:T(4,128)(2,1)} async-done(((bf16[3,256,768]{1,0,2:T(4,128)(2,1)}), bf16[3,256,768]{1,0,2:T(4,128)(2,1)}, u32[]{:S(2)}, u32[]{:S(2)}) %all-to-all-start) | async-done | bytes 1179680 | tf_op jit(solution)/shard_map/all_to_all | solution.py:154
  116.0 25.4 %all-to-all-done.2 = bf16[3,256,768]{1,0,2:T(4,128)(2,1)} async-done(((bf16[3,256,768]{1,0,2:T(4,128)(2,1)}), bf16[3,256,768]{1,0,2:T(4,128)(2,1)}, u32[]{:S(2)}, u32[]{:S(2)}) %all-to-all-start.2) | async-done | bytes 1179680 | tf_op jit(solution)/shard_map/all_to_all | solution.py:156
  153.6 43.8 %while.54 = (s32[]{:T(128)}, bf16[3,1024,192]{1,2,0:T(8,128)(2,1)}, f32[3,2,3,512]{3,2,1,0:T(4,128)}, bf16[3,1024,3,64]{1,3,2,0:T(8,128)(2,1)}, bf16[3,1024,3,64...) while((s32[]{:T(128)}, bf16[3,1024,192]{1,2,0:T(8,128)(2,1)}, ...), condition=%wide.region_7.8_spmd, body=%wide.region_2.7_spmd.sunk | while | flops 420051456 | bytes 28114308 | solution.py:166
  156.9 8.6 while.57
  171.5 8.6 while.57
  186.0 8.6 while.57
  201.6 51.3 %all_to_all.108 = bf16[3,1024,192]{2,0,1:T(4,128)(2,1)S(1)} all-to-all(bf16[3,1024,192]{2,0,1:T(4,128)(2,1)} %copy.117), channel_id=1, replica_groups=mesh['dp'=8,'seq'=4] {'seq'}, dimensions={1} | all-to-all | bytes 2359296 | tf_op jit(solution)/shard_map/all_to_all | solution.py:170
  269.6 27.3 %convert_reduce_fusion = (f32[3072]{0:T(1024)}, bf16[768,3072]{1,0:T(8,128)(2,1)S(1)}, f32[768,3072]{1,0:T(8,128)}) fusion(f32[768,3072]{1,0:T(8,128)S(1)} %fusion.73, f32[3072]{0:T(1024)S(1)} %copy-done.58, bf16[768,768]{1,0:T(8,128)(2,1)S(1)} %bitcast.247, bf16[3072,768]{1,0:T(8,128)(2,1)S(1)} %bitcast.262), kind=kOutput, calls=%fused_computation.74 | convolution fusion | flops 3800822784 | bytes 29515776 | tf_op jit(solution)/shard_map/dot_general | solution.py:22
  311.3 36.0 %all-to-all-done.4 = bf16[3,256,768]{1,0,2:T(4,128)(2,1)S(1)} async-done(((bf16[3,256,768]{1,0,2:T(4,128)(2,1)}), bf16[3,256,768]{1,0,2:T(4,128)(2,1)S(1)}, u32[]{:S(2)}, u32[]{:S(2)}) %all-to-all-start.4) | async-done | bytes 1179680 | tf_op jit(solution)/shard_map/all_to_all | solution.py:197
  352.8 180.7 %while.56 = (s32[]{:T(128)}, bf16[3,1024,192]{1,2,0:T(8,128)(2,1)}, bf16[3,1024,192]{1,2,0:T(8,128)(2,1)}, bf16[3,1024,192]{1,2,0:T(8,128)(2,1)}, bf16[3,1024,3,...) while((s32[]{:T(128)}, bf16[3,1024,192]{1,2,0:T(8,128)(2,1)}, ...), condition=%wide.region_16.17_spmd, body=%wide.region_12.16_spmd.sunk | while | flops 1034713664 | bytes 145711024 | solution.py:200
  359.7 48.1 %while.58 = (s32[]{:T(128)}, f32[1024,3,64]{0,2,1:T(8,128)S(1)}, f32[1024,3,64]{0,2,1:T(8,128)}, f32[2,512,3,64]{1,0,3,2:T(2,128)}, bf16[2,512,3,64]{1,3,2,0:T(8...) while((s32[]{:T(128)}, f32[1024,3,64]{0,2,1:T(8,128)S(1)}, ...), condition=%wide.region_15.15_spmd.clone, body=%wide.region_13.14_spmd.clone.sunk | while | flops 1031305728 | bytes 117228824 | solution.py:109
  420.0 48.1 %while.58 = (s32[]{:T(128)}, f32[1024,3,64]{0,2,1:T(8,128)S(1)}, f32[1024,3,64]{0,2,1:T(8,128)}, f32[2,512,3,64]{1,0,3,2:T(2,128)}, bf16[2,512,3,64]{1,3,2,0:T(8...) while((s32[]{:T(128)}, f32[1024,3,64]{0,2,1:T(8,128)S(1)}, ...), condition=%wide.region_15.15_spmd.clone, body=%wide.region_13.14_spmd.clone.sunk | while | flops 1031305728 | bytes 117228824 | solution.py:109
  435.8 8.0 dynamic_update_slice.50
  480.2 48.1 %while.58 = (s32[]{:T(128)}, f32[1024,3,64]{0,2,1:T(8,128)S(1)}, f32[1024,3,64]{0,2,1:T(8,128)}, f32[2,512,3,64]{1,0,3,2:T(2,128)}, bf16[2,512,3,64]{1,3,2,0:T(8...) while((s32[]{:T(128)}, f32[1024,3,64]{0,2,1:T(8,128)S(1)}, ...), condition=%wide.region_15.15_spmd.clone, body=%wide.region_13.14_spmd.clone.sunk | while | flops 1031305728 | bytes 117228824 | solution.py:109
  546.2 43.7 %all-to-all-done.7 = bf16[3,1024,192]{2,0,1:T(4,128)(2,1)} async-done(((bf16[3,1024,192]{2,0,1:T(4,128)(2,1)}), bf16[3,1024,192]{2,0,1:T(4,128)(2,1)}, u32[]{:S(2)}, u32[]{:S(2)}) %all-to-all-start.7) | async-done | bytes 1179680 | tf_op jit(solution)/shard_map/all_to_all | solution.py:207
  594.6 10.9 convolution_bitcast_fusion
  605.5 11.0 multiply_convert_fusion.1
  619.0 23.2 %all-to-all-done.5 = bf16[3,1024,192]{2,0,1:T(4,128)(2,1)} async-done(((bf16[3,1024,192]{2,0,1:T(4,128)(2,1)}), bf16[3,1024,192]{2,0,1:T(4,128)(2,1)}, u32[]{:S(2)}, u32[]{:S(2)}) %all-to-all-start.5) | async-done | bytes 1179680 | tf_op jit(solution)/shard_map/all_to_all | solution.py:205
  654.4 9.7 copy.130
  664.1 8.5 fusion.84
  672.6 10.7 reshape.502
  732.2 436.6 %all-reduce.10.cloned.1.call-done = (f32[589824]{0:T(1024)}, f32[589824]{0:T(1024)}, f32[589824]{0:T(1024)}, f32[589824]{0:T(1024)}, f32[2359296]{0:T(1024)}, /*index=5*/f32[2359296]{0:T(1024)}) async-done(((f32[589824]{0:T(1024)}, f32[589824]{0:T(1024)}, f32[589824]{0:T(1024)}, f32[589824]{0:T(1024)}, f32[2359296]{0:T(1024)}, /*index=5*/f32[2359296]{0:T(1024)}), (f32[589824]{0:T(1024)}, f32[589824]{0:T(1024)}, ...) | async-done | bytes 28311568
  1180.3 9.4 add_convert_fusion.4
  1199.9 41.9 %all-reduce.6 = (f32[768]{0:T(1024)}, f32[768]{0:T(1024)}, f32[768]{0:T(1024)}, f32[768]{0:T(1024)}, f32[768]{0:T(1024)}, /*index=5*/f32[768]{0:T(1024)}, f32[76...) all-reduce(f32[768]{0:T(1024)S(1)} %get-tuple-element.328, ...), channel_id=1, replica_groups=mesh['dp'=8,'seq'=4] {'dp','seq'}, use_global_device_ids=true, to_apply=%region_20.21 | all-reduce | flops 10054 | bytes 80432 | tf_op jit(solution)/shard_map/psum | solution.py:243
  1249.9 38.9 %all-gather.9.cloned.1.call-done = f32[589824]{0:T(1024)} async-done(((f32[18432]{0:T(1024)}), f32[589824]{0:T(1024)}) %all-gather.9.cloned.1.call-update) | async-done | bytes 2359312 | tf_op jit(solution)/shard_map/all_gather | solution.py:275
  1292.1 55.6 %all-gather.11.cloned.1.call-done = f32[589824]{0:T(1024)} async-done(((f32[18432]{0:T(1024)}), f32[589824]{0:T(1024)}) %all-gather.11.cloned.1.call-update) | async-done | bytes 2359312 | tf_op jit(solution)/shard_map/all_gather | solution.py:276
  1351.1 55.6 %all-gather.13.cloned.1.call-done = f32[589824]{0:T(1024)} async-done(((f32[18432]{0:T(1024)}), f32[589824]{0:T(1024)}) %all-gather.13.cloned.1.call-update) | async-done | bytes 2359312 | tf_op jit(solution)/shard_map/all_gather | solution.py:277
  1410.0 80.8 %all-gather.15.cloned.1.call-done = f32[2359296]{0:T(1024)} async-done(((f32[73728]{0:T(1024)}), f32[2359296]{0:T(1024)}) %all-gather.15.cloned.1.call-update) | async-done | bytes 9437200 | tf_op jit(solution)/shard_map/all_gather | solution.py:278
  1490.8 10.9 reshape.501
  1501.7 72.6 %all-gather.17.cloned.1.call-done = f32[2359296]{0:T(1024)} async-done(((f32[73728]{0:T(1024)}), f32[2359296]{0:T(1024)}) %all-gather.17.cloned.1.call-update) | async-done | bytes 9437200 | tf_op jit(solution)/shard_map/all_gather | solution.py:279
  1574.3 11.3 reshape.503
  (534 shorter events, 437.5 us)
Async XLA Ops:
  7.2 56.4 %copy-start = (bf16[768,768]{1,0:T(8,128)(2,1)S(1)}, bf16[768,768]{1,0:T(8,128)(2,1)}, u32[]{:S(2)}) copy-start(bf16[768,768]{1,0:T(8,128)(2,1)} %param.38) | copy-start | bytes 3538948
  15.9 43.3 %all-to-all-start.1 = ((bf16[3,256,768]{1,0,2:T(4,128)(2,1)}), bf16[3,256,768]{1,0,2:T(4,128)(2,1)S(1)}, u32[]{:S(2)}, u32[]{:S(2)}) async-start(bf16[3,256,768]{1,0,2:T(4,128)(2,1)} %copy.111), calls=%async_computation.1 | async-start | bytes 3145728 | tf_op jit(solution)/shard_map/all_to_all | solution.py:155
  26.0 37.6 %copy-start.71 = (f32[768]{0:T(1024)S(1)}, f32[768]{0:T(1024)}, u32[]{:S(2)}) copy-start(f32[768]{0:T(1024)} %param.39) | copy-start | bytes 9220
  59.2 40.9 %all-to-all-start = ((bf16[3,256,768]{1,0,2:T(4,128)(2,1)}), bf16[3,256,768]{1,0,2:T(4,128)(2,1)}, u32[]{:S(2)}, u32[]{:S(2)}) async-start(bf16[3,256,768]{1,0,2:T(4,128)(2,1)} %copy.108), calls=%async_computation | async-start | bytes 3145728 | tf_op jit(solution)/shard_map/all_to_all | solution.py:154
  66.9 38.0 %copy-start.65 = (s32[3]{0:T(128)S(1)}, s32[3]{0:T(128)}, u32[]{:S(2)}) copy-start(s32[3]{0:T(128)} %param.30) | copy-start | bytes 40
  100.1 41.3 %all-to-all-start.2 = ((bf16[3,256,768]{1,0,2:T(4,128)(2,1)}), bf16[3,256,768]{1,0,2:T(4,128)(2,1)}, u32[]{:S(2)}, u32[]{:S(2)}) async-start(bf16[3,256,768]{1,0,2:T(4,128)(2,1)} %copy.114), calls=%async_computation.2 | async-start | bytes 3145728 | tf_op jit(solution)/shard_map/all_to_all | solution.py:156
  197.4 55.5 %copy-start.7 = (bf16[3,1024,3,64]{1,3,2,0:T(8,128)(2,1)}, bf16[3,1024,3,64]{1,3,2,0:T(8,128)(2,1)S(1)}, u32[]{:S(2)}) copy-start(bf16[3,1024,3,64]{1,3,2,0:T(8,128)(2,1)S(1)} %get-tuple-element.910) | copy-start | bytes 3538948
  197.4 55.5 %copy-start.30 = (pred[3,1024]{1,0:T(4,128)(4,1)}, pred[3,1024]{1,0:T(4,128)(4,1)S(1)}, u32[]{:S(2)}) copy-start(pred[3,1024]{1,0:T(4,128)(4,1)S(1)} %get-tuple-element.943) | copy-start | bytes 9220
  261.6 40.2 %copy-start.8 = (f32[768,768]{1,0:T(8,128)}, f32[768,768]{1,0:T(8,128)S(1)}, u32[]{:S(2)}) copy-start(f32[768,768]{1,0:T(8,128)S(1)} %get-tuple-element.462) | copy-start | bytes 7077892
  261.7 40.1 %copy-start.35 = (f32[768]{0:T(1024)}, f32[768]{0:T(1024)S(1)}, u32[]{:S(2)}) copy-start(f32[768]{0:T(1024)S(1)} %broadcast_multiply_fusion) | copy-start | bytes 9220
  262.4 39.4 %copy-start.37 = (f32[768]{0:T(1024)}, f32[768]{0:T(1024)S(1)}, u32[]{:S(2)}) copy-start(f32[768]{0:T(1024)S(1)} %fusion.70) | copy-start | bytes 9220
  262.4 34.5 %slice-start = ((s8[4718592]{0:T(1024)(128)(4,1)}), s8[4194304]{0:T(1024)(128)(4,1)S(1)}, s32[]{:S(2)}) async-start(s8[4718592]{0:T(1024)(128)(4,1)} %bitcast.259), calls=%async_computation.15 | async-start | bytes 8388608
  269.5 27.4 %copy-start.13 = (f32[768,3072]{1,0:T(8,128)}, f32[768,3072]{1,0:T(8,128)S(1)}, u32[]{:S(2)}) copy-start(f32[768,3072]{1,0:T(8,128)S(1)} %fusion.73) | copy-start | bytes 28311556
  269.6 27.3 %slice-start.1 = ((s8[4718592]{0:T(1024)(128)(4,1)}), s8[524288]{0:T(1024)(128)(4,1)S(1)}, s32[]{:S(2)}) async-start(s8[4718592]{0:T(1024)(128)(4,1)} %bitcast.259), calls=%async_computation.16 | async-start | bytes 1048576
  307.3 40.0 %all-to-all-start.4 = ((bf16[3,256,768]{1,0,2:T(4,128)(2,1)}), bf16[3,256,768]{1,0,2:T(4,128)(2,1)S(1)}, u32[]{:S(2)}, u32[]{:S(2)}) async-start(bf16[3,256,768]{1,0,2:T(4,128)(2,1)} %copy.119), calls=%async_computation.4 | async-start | bytes 3145728 | tf_op jit(solution)/shard_map/all_to_all | solution.py:197
  537.5 52.3 %all-to-all-start.7 = ((bf16[3,1024,192]{2,0,1:T(4,128)(2,1)}), bf16[3,1024,192]{2,0,1:T(4,128)(2,1)}, u32[]{:S(2)}, u32[]{:S(2)}) async-start(bf16[3,1024,192]{2,0,1:T(4,128)(2,1)} %copy.126), calls=%async_computation.7 | async-start | bytes 4194304 | tf_op jit(solution)/shard_map/all_to_all | solution.py:207
  546.2 48.4 %copy-start.36 = (f32[768]{0:T(1024)S(1)}, f32[768]{0:T(1024)}, u32[]{:S(2)}) copy-start(f32[768]{0:T(1024)} %copy-done.35) | copy-start | bytes 9220
  546.2 48.4 %copy-start.38 = (f32[768]{0:T(1024)S(1)}, f32[768]{0:T(1024)}, u32[]{:S(2)}) copy-start(f32[768]{0:T(1024)} %copy-done.37) | copy-start | bytes 9220
  546.2 48.4 %copy-start.40 = (f32[768]{0:T(1024)S(1)}, f32[768]{0:T(1024)}, u32[]{:S(2)}) copy-start(f32[768]{0:T(1024)} %param.42) | copy-start | bytes 9220
  546.2 48.4 %copy-start.42 = (f32[768]{0:T(1024)S(1)}, f32[768]{0:T(1024)}, u32[]{:S(2)}) copy-start(f32[768]{0:T(1024)} %param.43) | copy-start | bytes 9220
  589.8 52.4 %all-to-all-start.5 = ((bf16[3,1024,192]{2,0,1:T(4,128)(2,1)}), bf16[3,1024,192]{2,0,1:T(4,128)(2,1)}, u32[]{:S(2)}, u32[]{:S(2)}) async-start(bf16[3,1024,192]{2,0,1:T(4,128)(2,1)} %copy.122), calls=%async_computation.5 | async-start | bytes 4194304 | tf_op jit(solution)/shard_map/all_to_all | solution.py:205
  619.0 27.8 %copy-start.25 = (bf16[768,768]{1,0:T(8,128)(2,1)S(1)}, bf16[768,768]{1,0:T(8,128)(2,1)}, u32[]{:S(2)}) copy-start(bf16[768,768]{1,0:T(8,128)(2,1)} %copy-done.24) | copy-start | bytes 3538948
  642.2 58.4 %all-to-all-start.6 = ((bf16[3,1024,192]{2,0,1:T(4,128)(2,1)}), bf16[3,1024,192]{2,0,1:T(4,128)(2,1)}, u32[]{:S(2)}, u32[]{:S(2)}) async-start(bf16[3,1024,192]{2,0,1:T(4,128)(2,1)} %copy.124), calls=%async_computation.6 | async-start | bytes 4194304 | tf_op jit(solution)/shard_map/all_to_all | solution.py:206
  646.7 522.1 %all-reduce.10.cloned.1.call-start = ((), (), s32[]{:S(2)}) async-start(), calls=%async_computation.14 | async-start | bytes 56623104
  732.1 447.3 %copy-start.63 = (s32[3,256]{1,0:T(4,128)S(1)}, s32[3,256]{1,0:T(4,128)}, u32[]{:S(2)}) copy-start(s32[3,256]{1,0:T(4,128)} %param.31) | copy-start | bytes 9220
  732.1 514.4 %all-gather.7.cloned.1.call-start = ((), (), s32[]{:S(2)}) async-start(), calls=%async_computation.8 | async-start | bytes 2433024 | tf_op jit(solution)/shard_map/all_gather | solution.py:274
  1170.3 118.5 %all-gather.9.cloned.1.call-start = ((), (), s32[]{:S(2)}) async-start(), calls=%async_computation.9 | async-start | bytes 2433024 | tf_op jit(solution)/shard_map/all_gather | solution.py:275
  1171.9 175.8 %all-gather.11.cloned.1.call-start = ((), (), s32[]{:S(2)}) async-start(), calls=%async_computation.10 | async-start | bytes 2433024 | tf_op jit(solution)/shard_map/all_gather | solution.py:276
  1173.5 233.1 %all-gather.13.cloned.1.call-start = ((), (), s32[]{:S(2)}) async-start(), calls=%async_computation.11 | async-start | bytes 2433024 | tf_op jit(solution)/shard_map/all_gather | solution.py:277
  1175.1 315.7 %all-gather.15.cloned.1.call-start = ((), (), s32[]{:S(2)}) async-start(), calls=%async_computation.12 | async-start | bytes 9732096 | tf_op jit(solution)/shard_map/all_gather | solution.py:278
  1176.9 397.4 %all-gather.17.cloned.1.call-start = ((), (), s32[]{:S(2)}) async-start(), calls=%async_computation.13 | async-start | bytes 9732096 | tf_op jit(solution)/shard_map/all_gather | solution.py:279
  1180.3 11.6 copy-start.26
  (102 other events, 321.3 us)
Sparse Core Ops, SparseCore 0:
  732.3 436.4 all-reduce.9
  1172.1 57.0 all-gather.6
  1232.6 56.1 all-gather.8
  1291.5 56.2 all-gather.10
  1350.4 56.2 all-gather.12
  1409.8 80.9 all-gather.14
  1493.6 80.6 all-gather.16
where the time goes:
time: 1600 us; the launch traced here: 1590 us
  waiting for transfers between devices  928 us (58%)
  local copies, waits for them, and re-layouts  257 us (16%)
  matrix products  188 us (12%)
  blocking collectives  93.2 us (6%)
  other arithmetic  77.4 us (5%)
  starting transfers between devices  33.4 us (2%)
    unnamed x8, waiting for transfers between devices  437 us
    all_gather x1, waiting for transfers between devices, on_device(): lax.all_gather(part_up, ('dp', 'seq'), axis=0, tiled=True)  80.8 us
    all_gather x1, waiting for transfers between devices, on_device(): lax.all_gather(part_down, ('dp', 'seq'), axis=0, tiled=True)  72.6 us
    all_gather x1, waiting for transfers between devices, on_device(): lax.all_gather(part_value, ('dp', 'seq'), axis=0, tiled=True)  55.6 us
    all_gather x1, waiting for transfers between devices, on_device(): lax.all_gather(part_out, ('dp', 'seq'), axis=0, tiled=True)  55.6 us
    all_to_all x1, blocking collectives, on_device(): lax.all_to_all(mixed, 'seq', split_axis=1, concat_axis=2, tiled=True)  51.3 us
    dynamic_update_slice x12, local copies, waits for them, and re-layouts, attend_backward(): lax.scan(visit, (start, start), (query_blocks, grad_blocks, logsum))  50.6 us
    all_to_all x1, waiting for transfers between devices, on_device(): lax.all_to_all(grad_value, 'seq', split_axis=1, concat_axis=2, tiled=True)  43.7 us
  transfers between devices with their start and end apart: 14, of which 12 were waited for; matrix products, arithmetic and copies ran while one was open for 10% of the time, Pallas kernels for 0%

commit v1 on v0

--- a/solution.py
+++ b/solution.py
@@ -153,7 +153,10 @@
     head_query, head_key, head_value = (
         lax.all_to_all(query, "seq", split_axis=2, concat_axis=1, tiled=True),
         lax.all_to_all(key, "seq", split_axis=2, concat_axis=1, tiled=True),
-        lax.all_to_all(value, "seq", split_axis=2, concat_axis=1, tiled=True),
+        jnp.concatenate(
+            lax.all_to_all(jnp.stack(jnp.split(value, lax.axis_size("seq"), axis=2)), "seq", 0, 0),
+            axis=1,
+        ),
     )
     count = head_query.shape[1]
     heads = head_query.shape[2] // HEAD

time: 1600 us -> 1600 us (level)
  transfers between devices with their start and end apart: 14 -> 14, of which waited for: 12 -> 12; matrix products, arithmetic and copies ran while one was open for 10% -> 11% of each run, Pallas kernels for 0% -> 0%
where the time goes in v1:
time: 1600 us; the launch traced here: 1580 us
  waiting for transfers between devices  915 us (57%)
  local copies, waits for them, and re-layouts  259 us (16%)
  matrix products  187 us (12%)
  blocking collectives  93.2 us (6%)
  other arithmetic  79.8 us (5%)
  starting transfers between devices  33.4 us (2%)
    unnamed x8, waiting for transfers between devices  437 us
    all_gather x1, waiting for transfers between devices, on_device(): lax.all_gather(part_up, ('dp', 'seq'), axis=0, tiled=True)  80.8 us
    all_gather x1, waiting for transfers between devices, on_device(): lax.all_gather(part_down, ('dp', 'seq'), axis=0, tiled=True)  72.6 us
    all_gather x1, waiting for transfers between devices, on_device(): lax.all_gather(part_value, ('dp', 'seq'), axis=0, tiled=True)  55.6 us
    all_gather x1, waiting for transfers between devices, on_device(): lax.all_gather(part_out, ('dp', 'seq'), axis=0, tiled=True)  55.6 us
    all_to_all x1, blocking collectives, on_device(): lax.all_to_all(mixed, 'seq', split_axis=1, concat_axis=2, tiled=True)  51.3 us
    dynamic_update_slice x12, local copies, waits for them, and re-layouts, attend_backward(): lax.scan(visit, (start, start), (query_blocks, grad_blocks, logsum))  50.7 us
    all_to_all x1, waiting for transfers between devices, on_device(): lax.all_to_all(grad_value, 'seq', split_axis=1, concat_axis=2, tiled=True)  43.7 us
  transfers between devices with their start and end apart: 14, of which 12 were waited for; matrix products, arithmetic and copies ran while one was open for 11% of the time, Pallas kernels for 0%

profile of v1, /device:TPU:0, one launch (start us, length us, event | category | flops | bytes accessed | tf_op | source)
XLA Modules:
  0.0 1584.2 jit_solution(11303392459551659057)
XLA Ops:
  29.5 29.6 %all-to-all-done.1 = bf16[3,256,768]{1,0,2:T(4,128)(2,1)S(1)} async-done(((bf16[3,256,768]{1,0,2:T(4,128)(2,1)}), bf16[3,256,768]{1,0,2:T(4,128)(2,1)S(1)}, u32[]{:S(2)}, u32[]{:S(2)}) %all-to-all-start.1) | async-done | bytes 1179680 | tf_op jit(solution)/shard_map/all_to_all | solution.py:155
  74.3 25.8 %all-to-all-done = bf16[3,256,768]{1,0,2:T(4,128)(2,1)} async-done(((bf16[3,256,768]{1,0,2:T(4,128)(2,1)}), bf16[3,256,768]{1,0,2:T(4,128)(2,1)}, u32[]{:S(2)}, u32[]{:S(2)}) %all-to-all-start) | async-done | bytes 1179680 | tf_op jit(solution)/shard_map/all_to_all | solution.py:154
  116.0 16.9 %all-to-all-done.2 = bf16[4,3,256,192]{2,3,1,0:T(8,128)(2,1)} async-done(((bf16[4,3,256,192]{2,3,1,0:T(8,128)(2,1)}), bf16[4,3,256,192]{2,3,1,0:T(8,128)(2,1)}, u32[]{:S(2)}, u32[]{:S(2)}) %all-to-all-start.2) | async-done | bytes 1179680 | tf_op jit(solution)/shard_map/all_to_all | solution.py:157
  144.8 43.8 %while.54 = (s32[]{:T(128)}, bf16[3,1024,192]{1,2,0:T(8,128)(2,1)}, f32[3,2,3,512]{3,2,1,0:T(4,128)}, bf16[3,1024,3,64]{1,3,2,0:T(8,128)(2,1)}, bf16[3,1024,3,64...) while((s32[]{:T(128)}, bf16[3,1024,192]{1,2,0:T(8,128)(2,1)}, ...), condition=%wide.region_7.8_spmd, body=%wide.region_2.7_spmd.sunk | while | flops 420051456 | bytes 28114308 | solution.py:169
  148.2 8.6 while.57
  162.7 8.6 while.57
  177.2 8.6 while.57
  192.9 51.3 %all_to_all.98 = bf16[3,1024,192]{2,0,1:T(4,128)(2,1)S(1)} all-to-all(bf16[3,1024,192]{2,0,1:T(4,128)(2,1)} %copy.146), channel_id=1, replica_groups=mesh['dp'=8,'seq'=4] {'seq'}, dimensions={1} | all-to-all | bytes 2359296 | tf_op jit(solution)/shard_map/all_to_all | solution.py:173
  260.8 27.3 %convert_reduce_fusion = (f32[3072]{0:T(1024)}, bf16[768,3072]{1,0:T(8,128)(2,1)S(1)}, f32[768,3072]{1,0:T(8,128)}) fusion(f32[768,3072]{1,0:T(8,128)S(1)} %fusion.73, f32[3072]{0:T(1024)S(1)} %copy-done.58, bf16[768,768]{1,0:T(8,128)(2,1)S(1)} %bitcast.249, bf16[3072,768]{1,0:T(8,128)(2,1)S(1)} %bitcast.267), kind=kOutput, calls=%fused_computation.74 | convolution fusion | flops 3800822784 | bytes 29515776 | tf_op jit(solution)/shard_map/dot_general | solution.py:22
  302.5 36.0 %all-to-all-done.4 = bf16[3,256,768]{1,0,2:T(4,128)(2,1)S(1)} async-done(((bf16[3,256,768]{1,0,2:T(4,128)(2,1)}), bf16[3,256,768]{1,0,2:T(4,128)(2,1)S(1)}, u32[]{:S(2)}, u32[]{:S(2)}) %all-to-all-start.4) | async-done | bytes 1179680 | tf_op jit(solution)/shard_map/all_to_all | solution.py:200
  344.0 181.1 %while.56 = (s32[]{:T(128)}, bf16[3,1024,192]{1,2,0:T(8,128)(2,1)}, bf16[3,1024,192]{1,2,0:T(8,128)(2,1)}, bf16[3,1024,192]{1,2,0:T(8,128)(2,1)}, bf16[3,1024,3,...) while((s32[]{:T(128)}, bf16[3,1024,192]{1,2,0:T(8,128)(2,1)}, ...), condition=%wide.region_16.17_spmd, body=%wide.region_12.16_spmd.sunk | while | flops 1034713664 | bytes 145711024 | solution.py:203
  351.0 48.2 %while.58 = (s32[]{:T(128)}, f32[1024,3,64]{0,2,1:T(8,128)S(1)}, f32[1024,3,64]{0,2,1:T(8,128)}, f32[2,512,3,64]{1,0,3,2:T(2,128)}, bf16[2,512,3,64]{1,3,2,0:T(8...) while((s32[]{:T(128)}, f32[1024,3,64]{0,2,1:T(8,128)S(1)}, ...), condition=%wide.region_15.15_spmd.clone, body=%wide.region_13.14_spmd.clone.sunk | while | flops 1031305728 | bytes 117228824 | solution.py:109
  391.2 8.0 dynamic_update_slice.50
  411.4 48.2 %while.58 = (s32[]{:T(128)}, f32[1024,3,64]{0,2,1:T(8,128)S(1)}, f32[1024,3,64]{0,2,1:T(8,128)}, f32[2,512,3,64]{1,0,3,2:T(2,128)}, bf16[2,512,3,64]{1,3,2,0:T(8...) while((s32[]{:T(128)}, f32[1024,3,64]{0,2,1:T(8,128)S(1)}, ...), condition=%wide.region_15.15_spmd.clone, body=%wide.region_13.14_spmd.clone.sunk | while | flops 1031305728 | bytes 117228824 | solution.py:109
  471.8 48.2 %while.58 = (s32[]{:T(128)}, f32[1024,3,64]{0,2,1:T(8,128)S(1)}, f32[1024,3,64]{0,2,1:T(8,128)}, f32[2,512,3,64]{1,0,3,2:T(2,128)}, bf16[2,512,3,64]{1,3,2,0:T(8...) while((s32[]{:T(128)}, f32[1024,3,64]{0,2,1:T(8,128)S(1)}, ...), condition=%wide.region_15.15_spmd.clone, body=%wide.region_13.14_spmd.clone.sunk | while | flops 1031305728 | bytes 117228824 | solution.py:109
  537.8 43.7 %all-to-all-done.7 = bf16[3,1024,192]{2,0,1:T(4,128)(2,1)} async-done(((bf16[3,1024,192]{2,0,1:T(4,128)(2,1)}), bf16[3,1024,192]{2,0,1:T(4,128)(2,1)}, u32[]{:S(2)}, u32[]{:S(2)}) %all-to-all-start.7) | async-done | bytes 1179680 | tf_op jit(solution)/shard_map/all_to_all | solution.py:210
  586.2 10.9 convolution_bitcast_fusion
  597.1 11.0 multiply_convert_fusion.1
  610.7 23.2 %all-to-all-done.5 = bf16[3,1024,192]{2,0,1:T(4,128)(2,1)} async-done(((bf16[3,1024,192]{2,0,1:T(4,128)(2,1)}), bf16[3,1024,192]{2,0,1:T(4,128)(2,1)}, u32[]{:S(2)}, u32[]{:S(2)}) %all-to-all-start.5) | async-done | bytes 1179680 | tf_op jit(solution)/shard_map/all_to_all | solution.py:208
  646.0 9.7 copy.163
  655.7 8.5 fusion.85
  664.3 10.7 reshape.501
  723.8 436.6 %all-reduce.10.cloned.1.call-done = (f32[589824]{0:T(1024)}, f32[589824]{0:T(1024)}, f32[589824]{0:T(1024)}, f32[589824]{0:T(1024)}, f32[2359296]{0:T(1024)}, /*index=5*/f32[2359296]{0:T(1024)}) async-done(((f32[589824]{0:T(1024)}, f32[589824]{0:T(1024)}, f32[589824]{0:T(1024)}, f32[589824]{0:T(1024)}, f32[2359296]{0:T(1024)}, /*index=5*/f32[2359296]{0:T(1024)}), (f32[589824]{0:T(1024)}, f32[589824]{0:T(1024)}, ...) | async-done | bytes 28311568
  1172.0 9.4 add_convert_fusion.4
  1191.6 41.9 %all-reduce.6 = (f32[768]{0:T(1024)}, f32[768]{0:T(1024)}, f32[768]{0:T(1024)}, f32[768]{0:T(1024)}, f32[768]{0:T(1024)}, /*index=5*/f32[768]{0:T(1024)}, f32[76...) all-reduce(f32[768]{0:T(1024)S(1)} %get-tuple-element.345, ...), channel_id=1, replica_groups=mesh['dp'=8,'seq'=4] {'dp','seq'}, use_global_device_ids=true, to_apply=%region_20.21 | all-reduce | flops 10054 | bytes 80432 | tf_op jit(solution)/shard_map/psum | solution.py:246
  1241.6 38.9 %all-gather.9.cloned.1.call-done = f32[589824]{0:T(1024)} async-done(((f32[18432]{0:T(1024)}), f32[589824]{0:T(1024)}) %all-gather.9.cloned.1.call-update) | async-done | bytes 2359312 | tf_op jit(solution)/shard_map/all_gather | solution.py:278
  1283.8 55.6 %all-gather.11.cloned.1.call-done = f32[589824]{0:T(1024)} async-done(((f32[18432]{0:T(1024)}), f32[589824]{0:T(1024)}) %all-gather.11.cloned.1.call-update) | async-done | bytes 2359312 | tf_op jit(solution)/shard_map/all_gather | solution.py:279
  1342.7 55.6 %all-gather.13.cloned.1.call-done = f32[589824]{0:T(1024)} async-done(((f32[18432]{0:T(1024)}), f32[589824]{0:T(1024)}) %all-gather.13.cloned.1.call-update) | async-done | bytes 2359312 | tf_op jit(solution)/shard_map/all_gather | solution.py:280
  1401.6 80.8 %all-gather.15.cloned.1.call-done = f32[2359296]{0:T(1024)} async-done(((f32[73728]{0:T(1024)}), f32[2359296]{0:T(1024)}) %all-gather.15.cloned.1.call-update) | async-done | bytes 9437200 | tf_op jit(solution)/shard_map/all_gather | solution.py:281
  1482.5 10.9 reshape.500
  1493.4 72.6 %all-gather.17.cloned.1.call-done = f32[2359296]{0:T(1024)} async-done(((f32[73728]{0:T(1024)}), f32[2359296]{0:T(1024)}) %all-gather.17.cloned.1.call-update) | async-done | bytes 9437200 | tf_op jit(solution)/shard_map/all_gather | solution.py:282
  1565.9 11.3 reshape.502
  (538 shorter events, 441.3 us)
Async XLA Ops:
  7.2 56.4 %copy-start = (bf16[768,768]{1,0:T(8,128)(2,1)S(1)}, bf16[768,768]{1,0:T(8,128)(2,1)}, u32[]{:S(2)}) copy-start(bf16[768,768]{1,0:T(8,128)(2,1)} %param.38) | copy-start | bytes 3538948
  15.9 43.3 %all-to-all-start.1 = ((bf16[3,256,768]{1,0,2:T(4,128)(2,1)}), bf16[3,256,768]{1,0,2:T(4,128)(2,1)S(1)}, u32[]{:S(2)}, u32[]{:S(2)}) async-start(bf16[3,256,768]{1,0,2:T(4,128)(2,1)} %copy.138), calls=%async_computation.1 | async-start | bytes 3145728 | tf_op jit(solution)/shard_map/all_to_all | solution.py:155
  26.0 37.6 %copy-start.71 = (f32[768]{0:T(1024)S(1)}, f32[768]{0:T(1024)}, u32[]{:S(2)}) copy-start(f32[768]{0:T(1024)} %param.39) | copy-start | bytes 9220
  59.2 40.9 %all-to-all-start = ((bf16[3,256,768]{1,0,2:T(4,128)(2,1)}), bf16[3,256,768]{1,0,2:T(4,128)(2,1)}, u32[]{:S(2)}, u32[]{:S(2)}) async-start(bf16[3,256,768]{1,0,2:T(4,128)(2,1)} %copy.135), calls=%async_computation | async-start | bytes 3145728 | tf_op jit(solution)/shard_map/all_to_all | solution.py:154
  72.0 32.9 %copy-start.65 = (s32[3]{0:T(128)S(1)}, s32[3]{0:T(128)}, u32[]{:S(2)}) copy-start(s32[3]{0:T(128)} %param.30) | copy-start | bytes 40
  100.1 32.8 %all-to-all-start.2 = ((bf16[4,3,256,192]{2,3,1,0:T(8,128)(2,1)}), bf16[4,3,256,192]{2,3,1,0:T(8,128)(2,1)}, u32[]{:S(2)}, u32[]{:S(2)}) async-start(bf16[4,3,256,192]{2,3,1,0:T(8,128)(2,1)} %pad_maximum_fusion.4), calls=%async_computation.2 | async-start | bytes 2359296 | tf_op jit(solution)/shard_map/all_to_all | solution.py:157
  188.6 55.5 %copy-start.7 = (bf16[3,1024,3,64]{1,3,2,0:T(8,128)(2,1)}, bf16[3,1024,3,64]{1,3,2,0:T(8,128)(2,1)S(1)}, u32[]{:S(2)}) copy-start(bf16[3,1024,3,64]{1,3,2,0:T(8,128)(2,1)S(1)} %get-tuple-element.931) | copy-start | bytes 3538948
  188.6 55.5 %copy-start.30 = (pred[3,1024]{1,0:T(4,128)(4,1)}, pred[3,1024]{1,0:T(4,128)(4,1)S(1)}, u32[]{:S(2)}) copy-start(pred[3,1024]{1,0:T(4,128)(4,1)S(1)} %get-tuple-element.964) | copy-start | bytes 9220
  252.8 40.2 %copy-start.8 = (f32[768,768]{1,0:T(8,128)}, f32[768,768]{1,0:T(8,128)S(1)}, u32[]{:S(2)}) copy-start(f32[768,768]{1,0:T(8,128)S(1)} %get-tuple-element.483) | copy-start | bytes 7077892
  252.9 40.1 %copy-start.35 = (f32[768]{0:T(1024)}, f32[768]{0:T(1024)S(1)}, u32[]{:S(2)}) copy-start(f32[768]{0:T(1024)S(1)} %broadcast_multiply_fusion) | copy-start | bytes 9220
  253.6 39.4 %copy-start.37 = (f32[768]{0:T(1024)}, f32[768]{0:T(1024)S(1)}, u32[]{:S(2)}) copy-start(f32[768]{0:T(1024)S(1)} %fusion.70) | copy-start | bytes 9220
  253.6 34.5 %slice-start = ((s8[4718592]{0:T(1024)(128)(4,1)}), s8[4194304]{0:T(1024)(128)(4,1)S(1)}, s32[]{:S(2)}) async-start(s8[4718592]{0:T(1024)(128)(4,1)} %bitcast.264), calls=%async_computation.15 | async-start | bytes 8388608
  260.8 27.4 %copy-start.13 = (f32[768,3072]{1,0:T(8,128)}, f32[768,3072]{1,0:T(8,128)S(1)}, u32[]{:S(2)}) copy-start(f32[768,3072]{1,0:T(8,128)S(1)} %fusion.73) | copy-start | bytes 28311556
  260.8 27.3 %slice-start.1 = ((s8[4718592]{0:T(1024)(128)(4,1)}), s8[524288]{0:T(1024)(128)(4,1)S(1)}, s32[]{:S(2)}) async-start(s8[4718592]{0:T(1024)(128)(4,1)} %bitcast.264), calls=%async_computation.16 | async-start | bytes 1048576
  298.6 40.0 %all-to-all-start.4 = ((bf16[3,256,768]{1,0,2:T(4,128)(2,1)}), bf16[3,256,768]{1,0,2:T(4,128)(2,1)S(1)}, u32[]{:S(2)}, u32[]{:S(2)}) async-start(bf16[3,256,768]{1,0,2:T(4,128)(2,1)} %copy.148), calls=%async_computation.4 | async-start | bytes 3145728 | tf_op jit(solution)/shard_map/all_to_all | solution.py:200
  529.2 52.4 %all-to-all-start.7 = ((bf16[3,1024,192]{2,0,1:T(4,128)(2,1)}), bf16[3,1024,192]{2,0,1:T(4,128)(2,1)}, u32[]{:S(2)}, u32[]{:S(2)}) async-start(bf16[3,1024,192]{2,0,1:T(4,128)(2,1)} %copy.155), calls=%async_computation.7 | async-start | bytes 4194304 | tf_op jit(solution)/shard_map/all_to_all | solution.py:210
  537.8 48.3 %copy-start.36 = (f32[768]{0:T(1024)S(1)}, f32[768]{0:T(1024)}, u32[]{:S(2)}) copy-start(f32[768]{0:T(1024)} %copy-done.35) | copy-start | bytes 9220
  537.8 48.3 %copy-start.38 = (f32[768]{0:T(1024)S(1)}, f32[768]{0:T(1024)}, u32[]{:S(2)}) copy-start(f32[768]{0:T(1024)} %copy-done.37) | copy-start | bytes 9220
  537.8 48.4 %copy-start.40 = (f32[768]{0:T(1024)S(1)}, f32[768]{0:T(1024)}, u32[]{:S(2)}) copy-start(f32[768]{0:T(1024)} %param.42) | copy-start | bytes 9220
  537.8 48.4 %copy-start.42 = (f32[768]{0:T(1024)S(1)}, f32[768]{0:T(1024)}, u32[]{:S(2)}) copy-start(f32[768]{0:T(1024)} %param.43) | copy-start | bytes 9220
  581.5 52.4 %all-to-all-start.5 = ((bf16[3,1024,192]{2,0,1:T(4,128)(2,1)}), bf16[3,1024,192]{2,0,1:T(4,128)(2,1)}, u32[]{:S(2)}, u32[]{:S(2)}) async-start(bf16[3,1024,192]{2,0,1:T(4,128)(2,1)} %copy.151), calls=%async_computation.5 | async-start | bytes 4194304 | tf_op jit(solution)/shard_map/all_to_all | solution.py:208
  610.7 27.7 %copy-start.25 = (bf16[768,768]{1,0:T(8,128)(2,1)S(1)}, bf16[768,768]{1,0:T(8,128)(2,1)}, u32[]{:S(2)}) copy-start(bf16[768,768]{1,0:T(8,128)(2,1)} %copy-done.24) | copy-start | bytes 3538948
  633.9 58.4 %all-to-all-start.6 = ((bf16[3,1024,192]{2,0,1:T(4,128)(2,1)}), bf16[3,1024,192]{2,0,1:T(4,128)(2,1)}, u32[]{:S(2)}, u32[]{:S(2)}) async-start(bf16[3,1024,192]{2,0,1:T(4,128)(2,1)} %copy.153), calls=%async_computation.6 | async-start | bytes 4194304 | tf_op jit(solution)/shard_map/all_to_all | solution.py:209
  638.4 522.1 %all-reduce.10.cloned.1.call-start = ((), (), s32[]{:S(2)}) async-start(), calls=%async_computation.14 | async-start | bytes 56623104
  723.8 447.3 %copy-start.63 = (s32[3,256]{1,0:T(4,128)S(1)}, s32[3,256]{1,0:T(4,128)}, u32[]{:S(2)}) copy-start(s32[3,256]{1,0:T(4,128)} %param.31) | copy-start | bytes 9220
  723.8 514.4 %all-gather.7.cloned.1.call-start = ((), (), s32[]{:S(2)}) async-start(), calls=%async_computation.8 | async-start | bytes 2433024 | tf_op jit(solution)/shard_map/all_gather | solution.py:277
  1162.0 118.5 %all-gather.9.cloned.1.call-start = ((), (), s32[]{:S(2)}) async-start(), calls=%async_computation.9 | async-start | bytes 2433024 | tf_op jit(solution)/shard_map/all_gather | solution.py:278
  1163.6 175.8 %all-gather.11.cloned.1.call-start = ((), (), s32[]{:S(2)}) async-start(), calls=%async_computation.10 | async-start | bytes 2433024 | tf_op jit(solution)/shard_map/all_gather | solution.py:279
  1165.2 233.1 %all-gather.13.cloned.1.call-start = ((), (), s32[]{:S(2)}) async-start(), calls=%async_computation.11 | async-start | bytes 2433024 | tf_op jit(solution)/shard_map/all_gather | solution.py:280
  1166.8 315.7 %all-gather.15.cloned.1.call-start = ((), (), s32[]{:S(2)}) async-start(), calls=%async_computation.12 | async-start | bytes 9732096 | tf_op jit(solution)/shard_map/all_gather | solution.py:281
  1168.6 397.4 %all-gather.17.cloned.1.call-start = ((), (), s32[]{:S(2)}) async-start(), calls=%async_computation.13 | async-start | bytes 9732096 | tf_op jit(solution)/shard_map/all_gather | solution.py:282
  1172.0 11.6 copy-start.26
  (102 other events, 324.3 us)
Sparse Core Ops, SparseCore 0:
  723.9 436.5 all-reduce.9
  1163.8 57.0 all-gather.6
  1224.2 56.1 all-gather.8
  1283.1 56.2 all-gather.10
  1342.0 56.2 all-gather.12
  1401.5 80.9 all-gather.14
  1485.3 80.6 all-gather.16
